TPU v7x, 32 devices: a whole 2x2x4 slice. The times are simulated.
32 devices in a mesh: dp: 4 (over y, core), seq: 8 (over z, x).
Axes of the slice: x: 2, y: 2, z: 4, core: 2. Of those that a mesh axis runs over, the one named last changes fastest.
Arguments:
- mixer_in: bfloat16 [4, 2048, 2560], P('dp', 'seq'), may hold values from -6 to 6
- step_raw: float32 [4, 40, 2048], P('dp', None, 'seq'), may hold values from -3 to 3
- key_proj: bfloat16 [4, 2048, 128], P('dp', 'seq'), may hold values from -0.3125 to 0.3125
- query_proj: bfloat16 [4, 2048, 128], P('dp', 'seq'), may hold values from -0.3125 to 0.3125
- codec_ids: int32 [4, 2048], P('dp', 'seq'), may hold values from 0 to 1023
- finger_ids: int32 [4, 2048], P('dp', 'seq'), may hold values from 0 to 4, as said below
- fret_ids: int32 [4, 2048], P('dp', 'seq'), may hold values from 0 to 24, as said below
- grad_out: bfloat16 [4, 2048, 2560], P('dp', 'seq'), may hold values from -12 to 12
- decay_log: float32 [40], replicated, may hold values from -16 to 1
- skip_gain: float32 [40], replicated, may hold values from 0.5 to 1.5
- codec_bias: float32 [40, 1024], replicated, may hold values from -1.75 to 1.75
- fret_bias: float32 [40, 25], replicated, may hold values from -1.75 to 1.75
- finger_damp: float32 [40, 5], replicated, may hold values from -1.4 to -0.4
Outputs:
- grad_mixer_in: bfloat16 [4, 2048, 2560], P('dp', 'seq')
- grad_step_raw: float32 [4, 40, 2048], P('dp', None, 'seq')
- grad_key_proj: bfloat16 [4, 2048, 128], P('dp', 'seq')
- grad_query_proj: bfloat16 [4, 2048, 128], P('dp', 'seq')
- grad_decay_log: float32 [40], replicated
- grad_skip_gain: float32 [40], replicated
- grad_codec_bias: float32 [40, 1024], replicated
- grad_fret_bias: float32 [40, 25], replicated
- grad_finger_damp: float32 [40, 5], replicated
Inputs may be any that keep to these rules, and one draw needn't show every extreme that they name: `finger_ids`: each sequence's finger and fret ids are constant over 4 runs of positions that follow one another; the 3 positions where a run begins are drawn afresh for every sequence, one of them at a multiple of 256 where the finger changes; other neighbouring runs may share ids. `fret_ids`: constant over the same runs as finger_ids.
All inputs are finite; a program needn't handle non-finite values.
Results may differ from a plain program's by a relative error of at most 0.0057.
Values sent between devices are 32-bit elements; how exact they have to be, the bound alone decides.
A program may use at most 192 MiB of HBM per device.

v0:
```python
import jax
import jax.numpy as jnp
from jax import lax
from jax.sharding import PartitionSpec as P

STRETCH = 256
block_heads = 8


def shifted(value, axis, by):
    count = lax.axis_size(axis)
    pairs = [(i, i + by) for i in range(count) if 0 <= i + by < count]
    return lax.ppermute(value, axis, pairs)


def entering_2(value, axis, join, neutral, backward):
    count, mine = (lax.axis_size(axis), lax.axis_index(axis))
    pieces = jax.tree.map(lambda part: lax.all_gather(part, axis), value)
    if backward:
        pieces = jax.tree.map(lambda part: part[::-1], pieces)
        mine = count - 1 - mine
    running = jax.tree.map(
        lambda part, zero: jnp.full_like(part, 0) + jnp.asarray(zero, part.dtype), value, neutral
    )

    def lap(position, running):
        longer = join(running, jax.tree.map(lambda part: part[position], pieces))
        return jax.tree.map(lambda new, old: jnp.where(position < mine, new, old), longer, running)

    return lax.fori_loop(0, count - 1, lap, running)


def product(form, left, right):
    return jnp.einsum(form, left, right, preferred_element_type=jnp.float32)


def combine(earlier, later):
    return (earlier[0] + later[0], jnp.exp(later[0])[:, None, None] * earlier[1] + later[1])


def advance(carry, parts):
    return (jnp.exp(parts[0])[:, None, None] * carry + parts[1], carry)


def fold_step(carry, parts):
    return (combine(carry, parts), None)


def stretch_state(mixer_stretch, key_stretch, step_stretch, cum_stretch):
    length = mixer_stretch.shape[0]
    head_count = step_stretch.shape[0]
    tail_weight = jnp.exp(cum_stretch[:, -1:] - cum_stretch) * step_stretch
    weighted = (mixer_stretch.reshape(length, head_count, -1) * tail_weight.T[:, :, None]).astype(
        jnp.bfloat16
    )
    return product("lhp,ln->hpn", weighted, key_stretch)


def stretch_pull(grad_stretch, query_stretch, cum_stretch):
    length = grad_stretch.shape[0]
    head_count = cum_stretch.shape[0]
    weighted = (
        grad_stretch.reshape(length, head_count, -1) * jnp.exp(cum_stretch).T[:, :, None]
    ).astype(jnp.bfloat16)
    return product("lhp,ln->hpn", weighted, query_stretch)


def stretch_grads(
    mixer_stretch,
    key_stretch,
    query_stretch,
    grad_stretch,
    step_stretch,
    cum_stretch,
    state_in,
    state_grad,
    skip_gain,
):
    length, feature_width = mixer_stretch.shape
    head_count = step_stretch.shape[0]
    groups = head_count // block_heads
    head_dim = feature_width // head_count
    state_dim = key_stretch.shape[1]
    row_index = jnp.arange(length)
    causal = row_index[:, None] >= row_index[None, :]
    gram_block = jnp.dot(query_stretch, key_stretch.T, preferred_element_type=jnp.float32)
    query_wide = query_stretch.astype(jnp.float32)

    def one_group(carry, parts):
        gram_grad, query_extra, key_extra = carry
        mixer_group, grad_group, step_group, cum_group, state_group, pull_group, skip_group = parts
        gap_log = cum_group[:, :, None] - cum_group[:, None, :]
        decay_part = jnp.exp(jnp.where(causal[None], gap_log, -jnp.inf))
        step_cols = step_group[:, None, :]
        weights = (gram_block[None] * decay_part * step_cols).astype(jnp.bfloat16)
        diag_grad = product("hij,ihp->jhp", weights, grad_group)
        grad_weights = product("ihp,jhp->hij", grad_group, mixer_group)
        masked = grad_weights * decay_part
        gram_grad = gram_grad + jnp.sum(masked * step_cols, axis=0)
        grad_step = jnp.sum(masked * gram_block[None], axis=1)
        row_cross = jnp.sum(masked * gram_block[None] * step_cols, axis=2)
        grad_cum = row_cross - step_group * grad_step
        state_low = state_group.astype(jnp.bfloat16)
        state_read = product("ihp,hpn->hin", grad_group, state_low)
        rise_factor = jnp.exp(cum_group)
        query_extra = query_extra + jnp.sum(rise_factor[:, :, None] * state_read, axis=0)
        grad_cum = grad_cum + rise_factor * jnp.sum(state_read * query_wide[None], axis=2)
        block_total = cum_group[:, -1]
        tail_decay = jnp.exp(block_total[:, None] - cum_group)
        tail_weight = tail_decay * step_group
        grad_low = pull_group.astype(jnp.bfloat16)
        pulled_rows = product("ln,hpn->lhp", key_stretch, grad_low)
        grad_tail = jnp.sum(mixer_group.astype(jnp.float32) * pulled_rows, axis=2).T
        mixed_state = product("lhp,hpn->hln", mixer_group, grad_low)
        key_extra = key_extra + jnp.sum(tail_weight[:, :, None] * mixed_state, axis=0)
        tail_grad = grad_tail * tail_weight
        total_grad = jnp.sum(tail_grad, axis=1) + jnp.exp(block_total) * jnp.sum(
            pull_group * state_group, axis=(1, 2)
        )
        grad_cum = grad_cum - tail_grad
        grad_cum = grad_cum.at[:, -1].add(total_grad)
        grad_step = grad_step + grad_tail * tail_decay
        grad_mixer = (
            diag_grad
            + tail_weight.T[:, :, None] * pulled_rows
            + skip_group[None, :, None] * grad_group.astype(jnp.float32)
        )
        return ((gram_grad, query_extra, key_extra), (grad_mixer, grad_step, grad_cum))

    parts = (
        mixer_stretch.reshape(length, groups, block_heads, head_dim).transpose(1, 0, 2, 3),
        grad_stretch.reshape(length, groups, block_heads, head_dim).transpose(1, 0, 2, 3),
        step_stretch.reshape(groups, block_heads, length),
        cum_stretch.reshape(groups, block_heads, length),
        state_in.reshape(groups, block_heads, head_dim, state_dim),
        state_grad.reshape(groups, block_heads, head_dim, state_dim),
        skip_gain.reshape(groups, block_heads),
    )
    start = (
        jnp.zeros((length, length), jnp.float32),
        jnp.zeros((length, state_dim), jnp.float32),
        jnp.zeros((length, state_dim), jnp.float32),
    )
    (gram_grad, query_extra, key_extra), (mixer_grads, step_grads, cum_grads) = lax.scan(
        one_group, start, parts
    )
    gram_low = gram_grad.astype(jnp.bfloat16)
    grad_query = jnp.dot(gram_low, key_stretch, preferred_element_type=jnp.float32) + query_extra
    grad_key = jnp.dot(gram_low.T, query_stretch, preferred_element_type=jnp.float32) + key_extra
    grad_mixer = mixer_grads.transpose(1, 0, 2, 3).reshape(length, feature_width)
    return (
        grad_mixer,
        grad_key,
        grad_query,
        step_grads.reshape(head_count, length),
        cum_grads.reshape(head_count, length),
    )


def shards(
    mixer_in,
    step_raw,
    key_proj,
    query_proj,
    codec_ids,
    finger_ids,
    fret_ids,
    grad_out,
    decay_log,
    skip_gain,
    codec_bias,
    fret_bias,
    finger_damp,
):
    tokens = mixer_in.shape[1]
    feature_width = mixer_in.shape[2]
    head_count = decay_log.shape[0]
    head_dim = feature_width // head_count
    state_dim = key_proj.shape[2]
    stretches = tokens // STRETCH
    highest = lax.Precision.HIGHEST
    fingers = finger_ids[0]
    frets = fret_ids[0]
    codec_row = codec_ids[0]
    latest = jnp.stack([fingers[-1], frets[-1]])
    before = shifted(latest, "seq", 1)
    prior_finger = jnp.concatenate([before[0:1], fingers[:-1]])
    prior_fret = jnp.concatenate([before[1:2], frets[:-1]])
    position = lax.axis_index("seq") * tokens + jnp.arange(tokens, dtype=jnp.int32)
    changed = ((fingers != prior_finger) | (frets != prior_fret)).astype(jnp.float32)
    onset_mask = jnp.where(position == 0, 0.0, changed)
    codec_hot = (
        jnp.arange(codec_bias.shape[1], dtype=jnp.int32)[:, None] == codec_row[None, :]
    ).astype(jnp.float32)
    fret_hot = (jnp.arange(fret_bias.shape[1], dtype=jnp.int32)[:, None] == frets[None, :]).astype(
        jnp.float32
    )
    finger_hot = (
        jnp.arange(finger_damp.shape[1], dtype=jnp.int32)[:, None] == fingers[None, :]
    ).astype(jnp.float32)
    pre_step = (
        step_raw[0]
        + jnp.dot(codec_bias, codec_hot, precision=highest)
        + jnp.dot(fret_bias, fret_hot, precision=highest)
    )
    step_size = jax.nn.softplus(pre_step)
    damping = jnp.dot(jax.nn.softplus(finger_damp), finger_hot, precision=highest)
    decay_rate = jnp.exp(decay_log)
    log_decay = -decay_rate[:, None] * step_size - onset_mask[None, :] * damping
    step_blocks = step_size.reshape(head_count, stretches, STRETCH).transpose(1, 0, 2)
    cum_blocks = jnp.cumsum(
        log_decay.reshape(head_count, stretches, STRETCH).transpose(1, 0, 2), axis=2
    )
    mixer_blocks = mixer_in[0].reshape(stretches, STRETCH, feature_width)
    grad_blocks = grad_out[0].reshape(stretches, STRETCH, feature_width)
    key_blocks = key_proj[0].reshape(stretches, STRETCH, state_dim)
    query_blocks = query_proj[0].reshape(stretches, STRETCH, state_dim)
    totals = cum_blocks[:, :, -1]
    states = lax.map(
        lambda items: stretch_state(*items), (mixer_blocks, key_blocks, step_blocks, cum_blocks)
    )
    block_pulls = lax.map(
        lambda items: stretch_pull(*items), (grad_blocks, query_blocks, cum_blocks)
    )
    empty_state = jnp.zeros((head_count, head_dim, state_dim), jnp.float32)
    empty_total = jnp.zeros((head_count,), jnp.float32)
    own_forward = lax.scan(fold_step, (empty_total, empty_state), (totals, states))[0]
    own_backward = lax.scan(
        fold_step, (empty_total, empty_state), (totals, block_pulls), reverse=True
    )[0]
    entering = entering_2(own_forward, "seq", combine, (empty_total, empty_state), False)[1]
    leaving = entering_2(own_backward, "seq", combine, (empty_total, empty_state), True)[1]
    state_ins = lax.scan(advance, entering, (totals, states))[1]
    state_grads = lax.scan(advance, leaving, (totals, block_pulls), reverse=True)[1]
    outcome = lax.map(
        lambda items: stretch_grads(*items, skip_gain),
        (
            mixer_blocks,
            key_blocks,
            query_blocks,
            grad_blocks,
            step_blocks,
            cum_blocks,
            state_ins,
            state_grads,
        ),
    )
    grad_mixer, grad_key, grad_query, grad_step, grad_cum = outcome
    grad_log = jnp.flip(jnp.cumsum(jnp.flip(grad_cum, 2), 2), 2)
    grad_log = grad_log.transpose(1, 0, 2).reshape(head_count, tokens)
    grad_step = grad_step.transpose(1, 0, 2).reshape(head_count, tokens)
    grad_pre = (grad_step - decay_rate[:, None] * grad_log) * jax.nn.sigmoid(pre_step)
    grad_decay = -decay_rate * jnp.sum(step_size * grad_log, axis=1)
    grad_damp = jnp.dot(
        -(onset_mask[None, :] * grad_log), finger_hot.T, precision=highest
    ) * jax.nn.sigmoid(finger_damp)
    grad_codec = jnp.dot(grad_pre, codec_hot.T, precision=highest)
    grad_fret = jnp.dot(grad_pre, fret_hot.T, precision=highest)
    grad_skip = product(
        "lhp,lhp->h",
        mixer_in[0].reshape(tokens, head_count, head_dim),
        grad_out[0].reshape(tokens, head_count, head_dim),
    )
    small_grads = (grad_skip, grad_decay, grad_damp, grad_codec, grad_fret)
    small_grads = lax.psum(
        (small_grads[0], small_grads[1], small_grads[2], small_grads[3], small_grads[4]),
        ("dp", "seq"),
    )
    grad_scale = (lax.axis_size("dp") * lax.axis_size("seq") * tokens) ** (-0.5)
    return (
        grad_mixer.astype(jnp.bfloat16),
        grad_pre[None],
        grad_key.astype(jnp.bfloat16),
        grad_query.astype(jnp.bfloat16),
        small_grads[1] * grad_scale,
        small_grads[0] * grad_scale,
        small_grads[3] * grad_scale,
        small_grads[4] * grad_scale,
        small_grads[2] * grad_scale,
    )


def solution(mesh):
    in_specs = (
        P("dp", "seq", None),
        P("dp", None, "seq"),
        P("dp", "seq", None),
        P("dp", "seq", None),
        P("dp", "seq"),
        P("dp", "seq"),
        P("dp", "seq"),
        P("dp", "seq", None),
        P(),
        P(),
        P(),
        P(),
        P(),
    )
    out_specs = (
        P("dp", "seq", None),
        P("dp", None, "seq"),
        P("dp", "seq", None),
        P("dp", "seq", None),
        P(),
        P(),
        P(),
        P(),
        P(),
    )
    return jax.shard_map(shards, mesh=mesh, in_specs=in_specs, out_specs=out_specs, check_vma=False)
```

profile of v0, /device:TPU:8, one launch (start us, length us, event | category | flops | bytes accessed | tf_op | source)
XLA Modules:
  0.0 605.4 jit_solution(9062517489203797136)
XLA Ops:
  11.1 3.4 collective-permute-start
  33.7 3.1 fusion.44
  37.0 16.9 %all-gather = f32[8,40,1]{1,2,0:T(1,128)S(1)} all-gather(f32[1,40,1]{1,2,0:T(1,128)S(1)} %copy.133), channel_id=2, replica_groups=mesh['dp'=4,'seq'=8] {'seq'}, dimensions={0}, use_global_device_ids=true | all-gather | bytes 1440 | tf_op jit(solution)/shard_map/all_gather | solution.py:18
  54.6 120.1 %all-gather.6.cloned.1.call-done = f32[320,64,128]{2,1,0:T(8,128)} async-done(((f32[40,64,128]{2,1,0:T(8,128)}), f32[320,64,128]{2,1,0:T(8,128)}) %all-gather.6.cloned.1.call-update) | async-done | bytes 10485776 | tf_op jit(solution)/shard_map/all_gather | solution.py:18
  174.6 11.8 %while.42 = (s32[]{:T(128)}, f32[40,64,128]{2,1,0:T(8,128)S(1)}, s32[]{:T(128)}, f32[8,40]{1,0:T(8,128)S(1)}, f32[8,40,64,128]{3,2,1,0:T(8,128)}, /*index=5*/s32[]{:T(128)}, s32[]{:T(128)}) while((s32[]{:T(128)}, f32[40,64,128]{2,1,0:T(8,128)S(1)}, s32[]{:T(128)}, f32[8,40]{1,0:T(8,128)S(1)}, f32[8,40,64,128]{3,2,1,0:T(8,128)}, ...), condition=%wide.region_3.4_spmd.clone, body=%wide.region_2.3_spmd.clone.sunk | while | flops 1310724 | bytes 3932745 | solution.py:30
  186.5 139.1 %all-gather.8.cloned.1.call-done = f32[320,64,128]{2,1,0:T(8,128)} async-done(((f32[40,64,128]{2,1,0:T(8,128)}), f32[320,64,128]{2,1,0:T(8,128)}) %all-gather.8.cloned.1.call-update) | async-done | bytes 10485776 | tf_op jit(solution)/shard_map/all_gather | solution.py:18
  325.5 10.2 %rev.14 = f32[8,40,64,128]{3,2,1,0:T(8,128)} reverse(f32[8,40,64,128]{3,2,1,0:T(8,128)} %bitcast.277), dimensions={0} | reverse | bytes 20971520 | tf_op jit(solution)/shard_map/rev | solution.py:20
  335.7 11.6 %while.43 = (s32[]{:T(128)}, f32[40,64,128]{2,1,0:T(8,128)S(1)}, s32[]{:T(128)}, f32[8,40]{1,0:T(8,128)S(1)}, f32[8,40,64,128]{3,2,1,0:T(8,128)}, /*index=5*/s32[]{:T(128)}, s32[]{:T(128)}) while((s32[]{:T(128)}, f32[40,64,128]{2,1,0:T(8,128)S(1)}, s32[]{:T(128)}, f32[8,40]{1,0:T(8,128)S(1)}, f32[8,40,64,128]{3,2,1,0:T(8,128)}, ...), condition=%wide.region_5.6_spmd.clone, body=%wide.region_4.5_spmd.clone.sunk | while | flops 1310724 | bytes 3932745 | solution.py:30
  347.3 116.2 %while.44 = (s32[]{:T(128)}, f32[256,256]{1,0:T(8,128)}, f32[256,128]{0,1:T(8,128)S(1)}, f32[256,128]{1,0:T(8,128)}, bf16[5,256,8,64]{1,3,2,0:T(8,128)(2,1)}, /*...) while((s32[]{:T(128)}, f32[256,256]{1,0:T(8,128)}, ...), condition=%wide.region_17.18_spmd.clone, body=%wide.region_7.17_spmd.clone.sunk | while | flops 245188640 | bytes 9993798 | solution.py:144
  350.9 3.1 multiply_reduce_fusion.13
  359.3 2.0 fusion.118
  364.0 2.6 fusion.117
  374.1 3.1 multiply_reduce_fusion.13
  382.5 2.0 fusion.118
  387.2 2.6 fusion.117
  397.3 3.1 multiply_reduce_fusion.13
  405.8 2.0 fusion.118
  410.5 2.6 fusion.117
  420.6 3.1 multiply_reduce_fusion.13
  433.7 2.6 fusion.117
  443.8 3.1 multiply_reduce_fusion.13
  457.0 2.6 fusion.117
  470.5 40.3 %all-reduce = (f32[40]{0:T(128)S(1)}, f32[40]{0:T(128)S(1)}, f32[40,25]{0,1:T(8,128)S(1)}, f32[40,5]{0,1:T(8,128)S(1)}) all-reduce(f32[40]{0:T(128)S(1)} %negate_multiply_fusion, f32[40]{0:T(128)S(1)} %copy-done.23, f32[40,25]{0,1:T(8,128)S(1)} %fusion.69, ...), channel_id=1, replica_groups=mesh['dp'=4,'seq'=8] {'dp','seq'}, use_global_device_ids=true, to_apply=%region_21.22 | all-reduce | flops 1280 | bytes 10240 | tf_op jit(solution)/shard_map/psum | solution.py:265
  516.0 81.3 %all-reduce.3.cloned.1.call-done = f32[40,1024]{1,0:T(8,128)} async-done(((f32[40,1024]{1,0:T(8,128)}), f32[40,1024]{1,0:T(8,128)}) %all-reduce.3.cloned.1.call-update) | async-done | bytes 163856 | tf_op jit(solution)/shard_map/psum | solution.py:265
  (298 shorter events, 141.4 us)
Async XLA Ops:
  7.2 10.2 %copy-start = (f32[40,1024]{1,0:T(8,128)S(1)}, f32[40,1024]{1,0:T(8,128)}, u32[]{:S(2)}) copy-start(f32[40,1024]{1,0:T(8,128)} %param.31) | copy-start | bytes 491524
  7.2 167.4 %all-gather.6.cloned.1.call-start = ((), (), s32[]{:S(2)}) async-start(), calls=%async_computation.1 | async-start | bytes 11796480 | tf_op jit(solution)/shard_map/all_gather | solution.py:18
  11.1 7.0 %collective-permute-start = (s32[2]{0:T(128)S(1)}, s32[2]{0:T(128)S(1)}, u32[]{:S(2)}, u32[]{:S(2)}) collective-permute-start(s32[2]{0:T(128)S(1)} %pad_add_fusion), channel_id=1, source_target_pairs={{0,1},{1,2},{2,3},{3,4},{4,5},{5,6},{6,7},{8,9},{9,10},{10,11},{11... | collective-permute-start | bytes 32 | tf_op jit(solution)/shard_map/ppermute | solution.py:13
  15.7 5.0 copy-start.21
  17.4 5.8 copy-start.1
  18.1 5.1 copy-start.14
  25.6 300.0 %all-gather.8.cloned.1.call-start = ((), (), s32[]{:S(2)}) async-start(), calls=%async_computation.2 | async-start | bytes 11796480 | tf_op jit(solution)/shard_map/all_gather | solution.py:18
  30.2 567.1 %all-reduce.3.cloned.1.call-start = ((), (), s32[]{:S(2)}) async-start(), calls=%async_computation | async-start | bytes 327680 | tf_op jit(solution)/shard_map/psum | solution.py:265
  350.9 3.2 copy-start.9
  366.6 3.2 copy-start.4
  366.6 3.3 copy-start.8
  374.0 3.2 copy-start.9
  389.8 3.3 copy-start.4
  389.8 3.4 copy-start.8
  413.0 3.3 copy-start.4
  413.0 3.4 copy-start.8
  436.3 3.3 copy-start.4
  436.3 3.4 copy-start.8
  459.5 3.3 copy-start.4
  459.6 3.4 copy-start.8
  463.5 7.0 %copy-start.27 = (f32[40]{0:T(128)S(1)}, f32[40]{0:T(128)}, u32[]{:S(2)}) copy-start(f32[40]{0:T(128)} %param.29) | copy-start | bytes 484
  463.5 7.0 %copy-start.23 = (f32[40]{0:T(128)S(1)}, f32[40]{0:T(128)}, u32[]{:S(2)}) copy-start(f32[40]{0:T(128)} %fusion.44) | copy-start | bytes 484
  463.5 48.6 %copy-start.11 = (bf16[5,256,8,64]{1,3,2,0:T(8,128)(2,1)S(1)}, bf16[5,256,8,64]{1,3,2,0:T(8,128)(2,1)}, u32[]{:S(2)}) copy-start(bf16[5,256,8,64]{1,3,2,0:T(8,128)(2,1)} %get-tuple-element.638) | copy-start | bytes 3932164
  466.8 47.0 %copy-start.15 = (f32[40,256]{1,0:T(8,128)}, f32[40,256]{1,0:T(8,128)S(1)}, u32[]{:S(2)}) copy-start(f32[40,256]{1,0:T(8,128)S(1)} %get-tuple-element.918) | copy-start | bytes 122884
  (32 other events, 60.3 us)
Sparse Core Ops, SparseCore 0:
  25.7 148.8 all-gather.5
  176.8 148.6 all-gather.7
  470.6 126.5 all-reduce.2
where the time goes:
time: 608 us; the launch traced here: 605 us
  waiting for transfers between devices  340 us (56%)
  other arithmetic  75.4 us (12%)
  matrix products  62.1 us (10%)
  blocking collectives  57.3 us (9%)
  local copies, waits for them, and re-layouts  51.5 us (8%)
  between operations  14.2 us (2%)
    all_gather x2, waiting for transfers between devices, entering_2(): pieces = jax.tree.map(lambda part: lax.all_gather(part, axis), value)  259 us
    psum x1, waiting for transfers between devices, shards(): lax.psum((small_grads[0], small_grads[1], small_grads[2], small_grads[3],...  81.3 us
    dot_general x27, matrix products, product(): return jnp.einsum(form, left, right, preferred_element_type=jnp.float32)  54.9 us
    psum x1, blocking collectives, shards(): lax.psum((small_grads[0], small_grads[1], small_grads[2], small_grads[3],...  40.3 us
    select_n x14, other arithmetic, lap(): jnp.where(position < mine, new, old)  22.9 us
    all_gather x1, blocking collectives, entering_2(): pieces = jax.tree.map(lambda part: lax.all_gather(part, axis), value)  16.9 us
  transfers between devices with their start and end apart: 4, of which 3 were waited for; matrix products, arithmetic and copies ran while one was open for 5% of the time, Pallas kernels for 0%

commit v1 on v0

--- a/solution.py
+++ b/solution.py
@@ -263,8 +263,10 @@
     )
     small_grads = (grad_skip, grad_decay, grad_damp, grad_codec, grad_fret)
     small_grads = lax.psum(
-        (small_grads[0], small_grads[1], small_grads[2], small_grads[3], small_grads[4]),
-        ("dp", "seq"),
+        lax.psum(
+            (small_grads[0], small_grads[1], small_grads[2], small_grads[3], small_grads[4]), "seq"
+        ),
+        "dp",
     )
     grad_scale = (lax.axis_size("dp") * lax.axis_size("seq") * tokens) ** (-0.5)
     return (

time: 608 us -> 632 us (1.039)
  waiting for transfers between devices: 340 us -> 359 us
    psum x0 -> x1, waiting for transfers between devices: none -> 33 us  [shards(): lax.psum(lax.psum((small_grads[0], small_grads[1], small_grads[2], small_...]
    psum x1, waiting for transfers between devices: 81.3 us -> 67.2 us  [shards(): lax.psum((small_grads[0], small_grads[1], small_grads[2], small_grads[3],...]
    psum x0 -> x1, blocking collectives: none -> 10.2 us  [shards(): lax.psum(lax.psum((small_grads[0], small_grads[1], small_grads[2], small_...]
    psum x1, blocking collectives: 40.3 us -> 33.3 us  [shards(): lax.psum((small_grads[0], small_grads[1], small_grads[2], small_grads[3],...]
  transfers between devices with their start and end apart: 4 -> 5, of which waited for: 3 -> 4; matrix products, arithmetic and copies ran while one was open for 5% -> 5% of each run, Pallas kernels for 0% -> 0%
where the time goes in v1:
time: 632 us; the launch traced here: 628 us
  waiting for transfers between devices  359 us (57%)
  other arithmetic  75.5 us (12%)
  matrix products  62.1 us (10%)
  blocking collectives  60.5 us (10%)
  local copies, waits for them, and re-layouts  51.5 us (8%)
  between operations  14.2 us (2%)
    all_gather x2, waiting for transfers between devices, entering_2(): pieces = jax.tree.map(lambda part: lax.all_gather(part, axis), value)  259 us
    psum x1, waiting for transfers between devices, shards(): lax.psum((small_grads[0], small_grads[1], small_grads[2], small_grads[3],...  67.2 us
    dot_general x27, matrix products, product(): return jnp.einsum(form, left, right, preferred_element_type=jnp.float32)  54.9 us
    psum x1, blocking collectives, shards(): lax.psum((small_grads[0], small_grads[1], small_grads[2], small_grads[3],...  33.3 us
    psum x1, waiting for transfers between devices, shards(): lax.psum(lax.psum((small_grads[0], small_grads[1], small_grads[2], small_...  33 us
    select_n x14, other arithmetic, lap(): jnp.where(position < mine, new, old)  22.9 us
    all_gather x1, blocking collectives, entering_2(): pieces = jax.tree.map(lambda part: lax.all_gather(part, axis), value)  16.9 us
  transfers between devices with their start and end apart: 5, of which 4 were waited for; matrix products, arithmetic and copies ran while one was open for 5% of the time, Pallas kernels for 0%

profile of v1, /device:TPU:8, one launch (start us, length us, event | category | flops | bytes accessed | tf_op | source)
XLA Modules:
  0.0 627.6 jit_solution(11020733291045165007)
XLA Ops:
  11.1 3.4 collective-permute-start
  33.7 3.1 fusion.44
  37.0 16.9 %all-gather = f32[8,40,1]{1,2,0:T(1,128)S(1)} all-gather(f32[1,40,1]{1,2,0:T(1,128)S(1)} %copy.133), channel_id=2, replica_groups=mesh['dp'=4,'seq'=8] {'seq'}, dimensions={0}, use_global_device_ids=true | all-gather | bytes 1440 | tf_op jit(solution)/shard_map/all_gather | solution.py:18
  54.6 120.1 %all-gather.6.cloned.1.call-done = f32[320,64,128]{2,1,0:T(8,128)} async-done(((f32[40,64,128]{2,1,0:T(8,128)}), f32[320,64,128]{2,1,0:T(8,128)}) %all-gather.6.cloned.1.call-update) | async-done | bytes 10485776 | tf_op jit(solution)/shard_map/all_gather | solution.py:18
  174.6 11.8 %while.42 = (s32[]{:T(128)}, f32[40,64,128]{2,1,0:T(8,128)S(1)}, s32[]{:T(128)}, f32[8,40]{1,0:T(8,128)S(1)}, f32[8,40,64,128]{3,2,1,0:T(8,128)}, /*index=5*/s32[]{:T(128)}, s32[]{:T(128)}) while((s32[]{:T(128)}, f32[40,64,128]{2,1,0:T(8,128)S(1)}, s32[]{:T(128)}, f32[8,40]{1,0:T(8,128)S(1)}, f32[8,40,64,128]{3,2,1,0:T(8,128)}, ...), condition=%wide.region_3.4_spmd.clone, body=%wide.region_2.3_spmd.clone.sunk | while | flops 1310724 | bytes 3932745 | solution.py:30
  186.5 139.1 %all-gather.8.cloned.1.call-done = f32[320,64,128]{2,1,0:T(8,128)} async-done(((f32[40,64,128]{2,1,0:T(8,128)}), f32[320,64,128]{2,1,0:T(8,128)}) %all-gather.8.cloned.1.call-update) | async-done | bytes 10485776 | tf_op jit(solution)/shard_map/all_gather | solution.py:18
  325.5 10.2 %rev.14 = f32[8,40,64,128]{3,2,1,0:T(8,128)} reverse(f32[8,40,64,128]{3,2,1,0:T(8,128)} %bitcast.277), dimensions={0} | reverse | bytes 20971520 | tf_op jit(solution)/shard_map/rev | solution.py:20
  335.7 11.6 %while.43 = (s32[]{:T(128)}, f32[40,64,128]{2,1,0:T(8,128)S(1)}, s32[]{:T(128)}, f32[8,40]{1,0:T(8,128)S(1)}, f32[8,40,64,128]{3,2,1,0:T(8,128)}, /*index=5*/s32[]{:T(128)}, s32[]{:T(128)}) while((s32[]{:T(128)}, f32[40,64,128]{2,1,0:T(8,128)S(1)}, s32[]{:T(128)}, f32[8,40]{1,0:T(8,128)S(1)}, f32[8,40,64,128]{3,2,1,0:T(8,128)}, ...), condition=%wide.region_5.6_spmd.clone, body=%wide.region_4.5_spmd.clone.sunk | while | flops 1310724 | bytes 3932745 | solution.py:30
  347.3 116.2 %while.44 = (s32[]{:T(128)}, f32[256,256]{1,0:T(8,128)}, f32[256,128]{0,1:T(8,128)S(1)}, f32[256,128]{1,0:T(8,128)}, bf16[5,256,8,64]{1,3,2,0:T(8,128)(2,1)}, /*...) while((s32[]{:T(128)}, f32[256,256]{1,0:T(8,128)}, ...), condition=%wide.region_17.18_spmd.clone, body=%wide.region_7.17_spmd.clone.sunk | while | flops 245188640 | bytes 9993798 | solution.py:144
  350.9 3.1 multiply_reduce_fusion.13
  359.3 2.0 fusion.118
  364.0 2.6 fusion.117
  374.1 3.1 multiply_reduce_fusion.13
  387.2 2.6 fusion.117
  397.3 3.1 multiply_reduce_fusion.13
  410.5 2.6 fusion.117
  420.6 3.1 multiply_reduce_fusion.13
  433.7 2.6 fusion.117
  443.8 3.1 multiply_reduce_fusion.13
  457.0 2.6 fusion.117
  470.5 33.3 %all-reduce = (f32[40]{0:T(128)S(1)}, f32[40]{0:T(128)S(1)}, f32[40,25]{0,1:T(8,128)S(1)}, f32[40,5]{0,1:T(8,128)S(1)}) all-reduce(f32[40]{0:T(128)S(1)} %negate_multiply_fusion, f32[40]{0:T(128)S(1)} %copy-done.23, f32[40,25]{0,1:T(8,128)S(1)} %fusion.69, ...), channel_id=1, replica_groups=mesh['dp'=4,'seq'=8] {'seq'}, use_global_device_ids=true, to_apply=%region_21.22 | all-reduce | flops 1280 | bytes 10240 | tf_op jit(solution)/shard_map/psum | solution.py:266
  503.8 10.2 %all-reduce.1 = (f32[40]{0:T(128)S(1)}, f32[40]{0:T(128)S(1)}, f32[40,25]{0,1:T(8,128)S(1)}, f32[40,5]{0,1:T(8,128)S(1)}) all-reduce(f32[40]{0:T(128)S(1)} %get-tuple-element.900, f32[40]{0:T(128)S(1)} %get-tuple-element.901, f32[40,25]{0,1:T(8,128)S(1)} %get-tuple-element.902, ...), channel_id=1, replica_groups=mesh['dp'=4,'seq'=8] {'dp'}, use_global_device_ids=true, to_apply=%region_22.23 | all-reduce | flops 1280 | bytes 10240 | tf_op jit(solution)/shard_map/psum | solution.py:265
  518.4 67.2 %all-reduce.5.cloned.1.call-done = f32[40,1024]{1,0:T(8,128)} async-done(((f32[40,1024]{1,0:T(8,128)}), f32[40,1024]{1,0:T(8,128)}) %all-reduce.5.cloned.1.call-update) | async-done | bytes 163856 | tf_op jit(solution)/shard_map/psum | solution.py:266
  586.5 33.0 %all-reduce.7.cloned.1.call-done = f32[40,1024]{1,0:T(8,128)} async-done(((f32[40,1024]{1,0:T(8,128)}), f32[40,1024]{1,0:T(8,128)}) %all-reduce.7.cloned.1.call-update) | async-done | bytes 163856 | tf_op jit(solution)/shard_map/psum | solution.py:265
  (302 shorter events, 145.5 us)
Async XLA Ops:
  7.2 10.2 %copy-start = (f32[40,1024]{1,0:T(8,128)S(1)}, f32[40,1024]{1,0:T(8,128)}, u32[]{:S(2)}) copy-start(f32[40,1024]{1,0:T(8,128)} %param.31) | copy-start | bytes 491524
  7.2 167.4 %all-gather.6.cloned.1.call-start = ((), (), s32[]{:S(2)}) async-start(), calls=%async_computation.2 | async-start | bytes 11796480 | tf_op jit(solution)/shard_map/all_gather | solution.py:18
  11.1 7.0 %collective-permute-start = (s32[2]{0:T(128)S(1)}, s32[2]{0:T(128)S(1)}, u32[]{:S(2)}, u32[]{:S(2)}) collective-permute-start(s32[2]{0:T(128)S(1)} %pad_add_fusion), channel_id=1, source_target_pairs={{0,1},{1,2},{2,3},{3,4},{4,5},{5,6},{6,7},{8,9},{9,10},{10,11},{11... | collective-permute-start | bytes 32 | tf_op jit(solution)/shard_map/ppermute | solution.py:13
  15.7 5.0 copy-start.21
  17.4 5.8 copy-start.1
  18.1 5.1 copy-start.14
  25.6 300.0 %all-gather.8.cloned.1.call-start = ((), (), s32[]{:S(2)}) async-start(), calls=%async_computation.3 | async-start | bytes 11796480 | tf_op jit(solution)/shard_map/all_gather | solution.py:18
  30.2 555.4 %all-reduce.5.cloned.1.call-start = ((), (), s32[]{:S(2)}) async-start(), calls=%async_computation | async-start | bytes 327680 | tf_op jit(solution)/shard_map/psum | solution.py:266
  366.6 3.3 copy-start.8
  389.8 3.3 copy-start.4
  389.8 3.4 copy-start.8
  413.0 3.3 copy-start.4
  413.0 3.4 copy-start.8
  436.3 3.3 copy-start.4
  436.3 3.4 copy-start.8
  459.5 3.3 copy-start.4
  459.6 3.4 copy-start.8
  463.5 6.9 %copy-start.27 = (f32[40]{0:T(128)S(1)}, f32[40]{0:T(128)}, u32[]{:S(2)}) copy-start(f32[40]{0:T(128)} %param.29) | copy-start | bytes 484
  463.5 6.9 %copy-start.23 = (f32[40]{0:T(128)S(1)}, f32[40]{0:T(128)}, u32[]{:S(2)}) copy-start(f32[40]{0:T(128)} %fusion.44) | copy-start | bytes 484
  463.5 52.4 %copy-start.11 = (bf16[5,256,8,64]{1,3,2,0:T(8,128)(2,1)S(1)}, bf16[5,256,8,64]{1,3,2,0:T(8,128)(2,1)}, u32[]{:S(2)}) copy-start(bf16[5,256,8,64]{1,3,2,0:T(8,128)(2,1)} %get-tuple-element.638) | copy-start | bytes 3932164
  467.7 49.9 %copy-start.15 = (f32[40,256]{1,0:T(8,128)}, f32[40,256]{1,0:T(8,128)S(1)}, u32[]{:S(2)}) copy-start(f32[40,256]{1,0:T(8,128)S(1)} %get-tuple-element.922) | copy-start | bytes 122884
  515.3 104.2 %all-reduce.7.cloned.1.call-start = ((), (), s32[]{:S(2)}) async-start(), calls=%async_computation.1 | async-start | bytes 327680 | tf_op jit(solution)/shard_map/psum | solution.py:265
  516.0 69.6 %copy-start.6 = (f32[256,128]{1,0:T(8,128)S(1)}, f32[256,128]{1,0:T(8,128)}, u32[]{:S(2)}) copy-start(f32[256,128]{1,0:T(8,128)} %get-tuple-element.642) | copy-start | bytes 393220
  516.0 69.6 %copy-start.13 = (bf16[1,256,128]{2,1,0:T(8,128)(2,1)S(1)}, bf16[1,256,128]{2,1,0:T(8,128)(2,1)}, u32[]{:S(2)}) copy-start(bf16[1,256,128]{2,1,0:T(8,128)(2,1)} %param.24) | copy-start | bytes 196612
  (33 other events, 63.5 us)
Sparse Core Ops, SparseCore 0:
  25.7 148.8 all-gather.5
  176.8 148.6 all-gather.7
  515.4 70.1 all-reduce.4
  587.8 31.6 all-reduce.6
